TPU v7x, 512 devices: a whole 4x4x16 slice. The times are simulated.
512 devices in a mesh: row: 32 (over x, z_lo, core), col: 16 (over z_hi, y).
Axes of the slice: x: 4, y: 4, z: 16 (z_hi: 4, z_lo: 4; z = z_hi * 4 + z_lo), core: 2. Of those that a mesh axis runs over, the one named last changes fastest.
Arguments:
- features: bfloat16 [65536, 512], P(('row', 'col')), may hold values from -6 to 6
- weight: bfloat16 [512, 512], replicated, may hold values from -0.25 to 0.25
- edge_tiles: bfloat16 [32, 16, 16, 3, 128, 128], P('row', 'col'), may hold values from -0.15625 to 0.15625
- tile_col: int32 [32, 16, 16, 3], P('row', 'col'), may hold values from 0 to 31, as said below
- tile_count: int32 [32, 16, 16], P('row', 'col'), may hold values from 0 to 3, as said below
- cotangent: bfloat16 [65536, 512], P(('row', 'col')), may hold values from -0.0234375 to 0.0234375
Outputs:
- activations: bfloat16 [65536, 512], P(('row', 'col'))
- weight_grad: float32 [512, 512], replicated
Inputs may be any that keep to these rules, and one draw needn't show every extreme that they name: `tile_col`: the live slots of one row block name different column blocks; slots that are not live hold arbitrary column blocks. Slots 0 to tile_count - 1 of a row block are live; the others hold arbitrary edge weights that are not part of the adjacency. Some row block holds 3 live slots.
All inputs are finite; a program needn't handle non-finite values.
Results may differ from a plain program's by a relative error of at most 0.024.
Values may be sent and summed in bfloat16 or wider, within the bound.
A program may use at most 64 MiB of HBM per device.

v0:
```python
import jax
import jax.numpy as jnp
from jax import lax
from jax.sharding import PartitionSpec as P


def local(features, weight, edge_tiles, tile_col, tile_count, cotangent):
    block_rows = features.shape[0]
    width_in = features.shape[1]
    row_blocks = edge_tiles.shape[2]
    slot_total = edge_tiles.shape[3]
    gathered = lax.all_gather(features, "row", axis=0, tiled=True)
    node_blocks = gathered.reshape(-1, block_rows, width_in)
    local_tiles = edge_tiles[0, 0]
    column_ids = tile_col[0, 0]
    live_counts = tile_count[0, 0]
    running = jnp.zeros((row_blocks, block_rows, width_in), jnp.float32)
    for slot in range(slot_total):
        picked = node_blocks[column_ids[:, slot]]
        product = jnp.einsum(
            "aij,ajf->aif", local_tiles[:, slot], picked, preferred_element_type=jnp.float32
        )
        is_live = (slot < live_counts)[:, None, None]
        running = running + jnp.where(is_live, product, 0.0)
    rounded_terms = running.reshape(row_blocks * block_rows, width_in).astype(jnp.bfloat16)
    owned = lax.psum_scatter(rounded_terms, "col", scatter_dimension=0, tiled=True).astype(
        jnp.float32
    )
    aggregated = owned.astype(jnp.bfloat16)
    preact = jnp.dot(aggregated, weight, preferred_element_type=jnp.float32)
    sigmoid_pre = jax.nn.sigmoid(preact)
    activations = (preact * sigmoid_pre).astype(jnp.bfloat16)
    pre_grad = (
        cotangent.astype(jnp.float32) * sigmoid_pre * (1.0 + preact * (1.0 - sigmoid_pre))
    ).astype(jnp.bfloat16)
    grad_term = lax.dot_general(
        aggregated, pre_grad, (((0,), (0,)), ((), ())), preferred_element_type=jnp.float32
    )
    weight_grad = lax.psum(grad_term, ("row", "col"))
    return (activations, weight_grad)


def solution(mesh):
    return jax.shard_map(
        local,
        mesh=mesh,
        in_specs=(
            P(("row", "col"), None),
            P(),
            P("row", "col", None, None, None, None),
            P("row", "col", None, None),
            P("row", "col", None),
            P(("row", "col"), None),
        ),
        out_specs=(P(("row", "col"), None), P()),
        check_vma=False,
    )
```

profile of v0, /device:TPU:1, one launch (start us, length us, event | category | flops | bytes accessed | tf_op | source)
XLA Modules:
  0.0 704.8 jit_solution(2866905184470524160)
XLA Ops:
  7.2 0.0 copy-start
  7.2 0.0 copy-start.3
  7.2 0.0 all-gather.2.cloned.1.call-start
  7.2 0.7 all-gather.2.cloned.1.call-update
  7.9 0.0 reduce-scatter.2.cloned.1.call-start
  8.0 0.7 copy.13
  8.7 2.8 copy.12
  11.5 0.0 copy-done.3
  11.5 72.5 %all-gather.2.cloned.1.call-done = bf16[4096,512]{1,0:T(8,128)(2,1)} async-done(((bf16[128,512]{1,0:T(8,128)(2,1)}), bf16[4096,512]{1,0:T(8,128)(2,1)}) %all-gather.2.cloned.1.call-update) | async-done | bytes 4194320 | tf_op jit(solution)/shard_map/all_gather | solution.py:12
  84.0 4.2 gather_fusion.2
  88.2 2.9 gather_fusion
  91.1 4.2 gather_fusion.1
  95.3 0.0 copy-start.2
  95.3 2.6 fusion
  97.8 0.0 copy-done.2
  97.8 0.0 copy-start.1
  97.8 0.7 fusion.1
  98.5 0.9 copy-done.1
  99.4 2.2 add_convert_fusion
  101.7 0.0 copy-start.4
  101.7 0.0 reduce-scatter.2.cloned.1.call-update
  101.7 0.0 all-reduce.2.cloned.1.call-start
  101.7 125.1 %reduce-scatter.2.cloned.1.call-done = bf16[128,512]{1,0:T(8,128)(2,1)} async-done(((bf16[2048,512]{1,0:T(8,128)(2,1)}), bf16[128,512]{1,0:T(8,128)(2,1)}) %reduce-scatter.2.cloned.1.call-update) | async-done | bytes 131088 | tf_op jit(solution)/shard_map/reduce_scatter | solution.py:26
  226.9 0.0 copy-done
  226.9 1.8 multiply_convert_fusion.1
  228.7 0.0 copy-done.4
  228.7 2.3 fusion.2
  231.0 0.0 all-reduce.2.cloned.1.call-update
  231.0 465.0 %all-reduce.2.cloned.1.call-done = f32[512,512]{1,0:T(8,128)} async-done(((f32[512,512]{1,0:T(8,128)}), f32[512,512]{1,0:T(8,128)}) %all-reduce.2.cloned.1.call-update) | async-done | bytes 1048592 | tf_op jit(solution)/shard_map/psum | solution.py:39
  696.0 2.3 copy.15
  (4 shorter events, 0.0 us)
Async XLA Ops:
  7.2 219.7 %copy-start = (bf16[512,512]{1,0:T(8,128)(2,1)S(1)}, bf16[512,512]{1,0:T(8,128)(2,1)}, u32[]{:S(2)}) copy-start(bf16[512,512]{1,0:T(8,128)(2,1)} %param.7) | copy-start | bytes 1572868
  7.2 4.3 copy-start.3
  7.2 76.8 %all-gather.2.cloned.1.call-start = ((), (), s32[]{:S(2)}) async-start(), calls=%async_computation.1 | async-start | bytes 4325376 | tf_op jit(solution)/shard_map/all_gather | solution.py:12
  7.9 219.0 %reduce-scatter.2.cloned.1.call-start = ((), (), s32[]{:S(2)}) async-start(), calls=%async_computation.2 | async-start | bytes 2228224 | tf_op jit(solution)/shard_map/reduce_scatter | solution.py:26
  95.3 2.6 copy-start.2
  97.8 1.6 copy-start.1
  101.7 127.0 %copy-start.4 = (bf16[128,512]{1,0:T(8,128)(2,1)S(1)}, bf16[128,512]{1,0:T(8,128)(2,1)}, u32[]{:S(2)}) copy-start(bf16[128,512]{1,0:T(8,128)(2,1)} %param.11) | copy-start | bytes 393220
  101.7 594.3 %all-reduce.2.cloned.1.call-start = ((), (), s32[]{:S(2)}) async-start(), calls=%async_computation.3 | async-start | bytes 2097152 | tf_op jit(solution)/shard_map/psum | solution.py:39
Sparse Core Ops, SparseCore 0:
  10.2 73.7 all-gather.1
  101.8 125.0 reduce-scatter.1
  233.8 462.1 all-reduce.1
where the time goes:
time: 705 us
  waiting for transfers between devices  663 us (94%)
  local copies, waits for them, and re-layouts  17.9 us (3%)
  between operations  13.8 us (2%)
  matrix products  9.59 us (1%)
    psum x1, waiting for transfers between devices, local(): weight_grad = lax.psum(grad_term, ('row', 'col'))  465 us
    reduce_scatter x1, waiting for transfers between devices, local(): lax.psum_scatter(rounded_terms, 'col', scatter_dimension=0, tiled=True)  125 us
    all_gather x1, waiting for transfers between devices, local(): gathered = lax.all_gather(features, 'row', axis=0, tiled=True)  72.5 us
  transfers between devices with their start and end apart: 3, of which 3 were waited for; matrix products, arithmetic and copies ran while one was open for 0% of the time, Pallas kernels for 0%

commit v1 on v0

v1 whole, which is shorter than its diff:
```python
import jax
import jax.numpy as jnp
from jax import lax
from jax.experimental import pallas as pl
from jax.experimental.pallas import tpu as pltpu
from jax.sharding import PartitionSpec as P

MESH = pl.DeviceIdType.MESH
BF, F32 = jnp.bfloat16, jnp.float32
N, W = 128, 512
CHUNKS = ((0, 128), (128, 128), (256, 128), (384, 128))
C = len(CHUNKS)


def device(x, zl, k, zh, y):
    return ((x * 4 + zl) * 2 + k, zh * 4 + y)


def turn(value, by):
    return lax.rem(value + (by + 16), 4)


def kernel(
    count_ref, col_ref, feat, edges, cot, weight, act_out, grad_out,
    *scratch,
):
    ag, te, r1, r2, su, sb, r3, r4 = (scratch[i * C : (i + 1) * C] for i in range(8))
    (raw, em, cv, wv, av, gv, own, sib, rsib, part, rxy, zown, rz, gz, gxy,
     in_sem, zs, zr, xs, xr, fs, fr, cs, cr, ys, yr, ys2, yr2, zs1, zr1, zs2, zr2, a_s, a_r) = scratch[8 * C :]
    row, col = lax.axis_index("row"), lax.axis_index("col")
    x, zl, k = row // 8, lax.rem(row // 2, 4), lax.rem(row, 2)
    zh, y = col // 4, lax.rem(col, 4)
    z = zh * 4 + zl
    sibling = device(x, zl, 1 - k, zh, y)

    def slot(core, at_x, at_zl=0):
        return core * 16 + at_x * 4 + at_zl

    def send(src, dst, send_sem, recv_sem, to):
        pltpu.make_async_remote_copy(
            src_ref=src, dst_ref=dst, send_sem=send_sem, recv_sem=recv_sem, device_id=to, device_id_type=MESH
        ).start()

    def wait(ref, sem):
        pltpu.make_async_copy(ref, ref, sem).wait()

    mine = slot(k, x, zl)
    loads = [
        pltpu.make_async_copy(feat.at[:, s : s + w], ag[f].at[mine], in_sem.at[f])
        for f, (s, w) in enumerate(CHUNKS)
    ]
    loads += [
        pltpu.make_async_copy(edges, raw, in_sem.at[C]),
        pltpu.make_async_copy(weight, wv, in_sem.at[C + 1]),
        pltpu.make_async_copy(cot, cv, in_sem.at[C + 2]),
    ]
    for load in loads:
        load.start()

    def xy_peer(i):
        return turn(x, i // 4), turn(y, i % 4)

    def z_peer(i):
        other = lax.rem(z + i, 16)
        return other

    barrier = pltpu.get_barrier_semaphore()
    pl.semaphore_signal(barrier, inc=1, device_id=sibling, device_id_type=MESH)
    for i in range(1, 16):
        px, py = xy_peer(i)
        pl.semaphore_signal(barrier, inc=1, device_id=device(px, zl, k, zh, py), device_id_type=MESH)
        pz = z_peer(i)
        pl.semaphore_signal(barrier, inc=1, device_id=device(x, lax.rem(pz, 4), k, pz // 4, y), device_id_type=MESH)
    pl.semaphore_wait(barrier, 31)

    right, left = device(turn(x, 1), zl, k, zh, y), device(turn(x, -1), zl, k, zh, y)

    def gather_z(f):
        loads[f].wait()
        for dz in range(1, 4):
            ref = ag[f].at[mine]
            send(ref, ref, zs.at[f], zr.at[f], device(x, turn(zl, dz), k, zh, y))

    def to_sibling(f, first, n):
        ref = ag[f].at[pl.ds(first, n)]
        send(ref, ref, cs.at[f], cr.at[f], sibling)

    def gather_x(f):
        wait(ag[f].at[pl.ds(0, 3)], zr.at[f])
        ref = ag[f].at[pl.ds(slot(k, x), 4)]
        send(ref, ref, xs.at[f], xr.at[f, 0], right)
        send(ref, ref, xs.at[f], xr.at[f, 1], left)
        to_sibling(f, slot(k, x), 4)

    def gather_on(f):
        lx, rx = turn(x, -1), turn(x, 1)
        wait(ag[f].at[pl.ds(0, 4)], xr.at[f, 0])
        ref = ag[f].at[pl.ds(slot(k, lx), 2)]
        send(ref, ref, fs.at[f], fr.at[f], right)
        wait(ag[f].at[pl.ds(0, 4)], xr.at[f, 1])
        ref = ag[f].at[pl.ds(slot(k, rx, 2), 2)]
        send(ref, ref, fs.at[f], fr.at[f], left)
        to_sibling(f, slot(k, lx), 4)
        to_sibling(f, slot(k, rx), 4)

    def gather_end(f):
        wait(ag[f].at[pl.ds(0, 4)], fr.at[f])
        to_sibling(f, slot(k, turn(x, 2)), 4)

    def mask_tiles():
        loads[C].wait()

        def one(a, _):
            count = count_ref[0, a]
            for s in range(3):
                tile = raw[a, s]
                em[a, :, s * N : (s + 1) * N] = jnp.where(s < count, tile, jnp.zeros_like(tile))
            return _

        lax.fori_loop(0, 16, one, 0)

    def terms(f, to_y):
        for q in range(4):
            a = q * 4 + to_y
            picked = []
            for s in range(3):
                j = col_ref[a, s]
                picked.append(ag[f][lax.rem(j, 2) * 16 + j // 2])
            made = jnp.dot(em[a], jnp.concatenate(picked, axis=0), preferred_element_type=F32)
            te[f][to_y * 4 + q] = made.astype(BF)

    up, down = device(x, zl, k, zh, turn(y, 1)), device(x, zl, k, zh, turn(y, -1))
    y_up, y_down, y_far = turn(y, 1), turn(y, -1), turn(y, 2)

    def multiply(f):
        wait(ag[f].at[pl.ds(0, 16)], cr.at[f])
        terms(f, y_far)
        send(te[f].at[pl.ds(y_far * 4, 2)], r1[f].at[0], ys.at[f], yr.at[f, 0], up)
        send(te[f].at[pl.ds(y_far * 4 + 2, 2)], r1[f].at[1], ys.at[f], yr.at[f, 1], down)
        terms(f, y_up)
        send(te[f].at[pl.ds(y_up * 4 + 2, 2)], r2[f].at[0, pl.ds(2, 2)], ys2.at[f], yr2.at[f], up)
        terms(f, y_down)
        send(te[f].at[pl.ds(y_down * 4, 2)], r2[f].at[1, pl.ds(0, 2)], ys2.at[f], yr2.at[f], down)
        terms(f, y)

    def reduce_y(f):
        wait(r1[f].at[0], yr.at[f, 0])
        at = pl.ds(y_up * 4, 2)
        te[f][at] = (te[f][at].astype(F32) + r1[f][0].astype(F32)).astype(BF)
        send(te[f].at[at], r2[f].at[0, pl.ds(0, 2)], ys2.at[f], yr2.at[f], up)
        wait(r1[f].at[1], yr.at[f, 1])
        at = pl.ds(y_down * 4 + 2, 2)
        te[f][at] = (te[f][at].astype(F32) + r1[f][1].astype(F32)).astype(BF)
        send(te[f].at[at], r2[f].at[1, pl.ds(2, 2)], ys2.at[f], yr2.at[f], down)

    z_up, z_down, z_far = turn(zh, 1), turn(zh, -1), turn(zh, 2)
    above, below = device(x, zl, k, z_up, y), device(x, zl, k, z_down, y)

    def reduce_y_end(f):
        wait(r2[f], yr2.at[f])

        def total(q):
            return te[f][y * 4 + q].astype(F32) + r2[f][0, q].astype(F32) + r2[f][1, q].astype(F32)

        sb[f][z_far] = total(z_far).astype(BF)
        send(sb[f].at[z_far, pl.ds(0, 64)], r3[f].at[0], zs1.at[f], zr1.at[f, 0], above)
        send(sb[f].at[z_far, pl.ds(64, 64)], r3[f].at[1], zs1.at[f], zr1.at[f, 1], below)
        for q in (z_up, z_down, zh):
            su[f][q] = total(q)

    def reduce_z(f):
        wait(r3[f].at[0], zr1.at[f, 0])
        sb[f][z_up, 0:64] = (su[f][z_up, 0:64] + r3[f][0].astype(F32)).astype(BF)
        sb[f][z_up, 64:128] = su[f][z_up, 64:128].astype(BF)
        send(sb[f].at[z_up], r4[f].at[0], zs2.at[f], zr2.at[f], above)
        wait(r3[f].at[1], zr1.at[f, 1])
        sb[f][z_down, 64:128] = (su[f][z_down, 64:128] + r3[f][1].astype(F32)).astype(BF)
        sb[f][z_down, 0:64] = su[f][z_down, 0:64].astype(BF)
        send(sb[f].at[z_down], r4[f].at[1], zs2.at[f], zr2.at[f], below)

    def reduce_z_end(f):
        wait(r4[f], zr2.at[f])
        s, w = CHUNKS[f]
        av[:, s : s + w] = (su[f][zh] + r4[f][0].astype(F32) + r4[f][1].astype(F32)).astype(BF)

    for f in range(C):
        gather_z(f)
    for t in range(C + 6):
        if t < C:
            gather_x(t)
        if t == 1:
            mask_tiles()
        if 0 <= t - 1 < C:
            gather_on(t - 1)
        if 0 <= t - 3 < C:
            reduce_y(t - 3)
        if 0 <= t - 4 < C:
            reduce_y_end(t - 4)
        if 0 <= t - 5 < C:
            reduce_z(t - 5)
        if 0 <= t - 6 < C:
            reduce_z_end(t - 6)
        if 0 <= t - 2 < C:
            gather_end(t - 2)
            multiply(t - 2)

    loads[C + 1].wait()
    loads[C + 2].wait()
    preact = jnp.dot(av[...], wv[...], preferred_element_type=F32)
    sig = jax.nn.sigmoid(preact)
    gv[...] = (cv[...].astype(F32) * sig * (1.0 + preact * (1.0 - sig))).astype(BF)
    act_out[...] = (preact * sig).astype(BF)

    def share(half):
        rows = av[:, pl.ds(pl.multiple_of(half * 256, 256), 256)]
        made = lax.dot_general(rows, gv[...], (((0,), (0,)), ((), ())), preferred_element_type=F32)
        return made.reshape(16, 16, W)

    sib[...] = share(1 - k).astype(BF)
    send(sib, rsib, a_s.at[0], a_r.at[0], sibling)
    own[...] = share(k)
    wait(rsib, a_r.at[0])
    own[...] = own[...] + rsib[...].astype(F32)
    part[...] = own[...].astype(BF)

    place = x * 4 + y
    for i in range(1, 16):
        px, py = xy_peer(i)
        send(part.at[px * 4 + py], rxy.at[i - 1], a_s.at[1], a_r.at[1], device(px, zl, k, zh, py))
    wait(rxy, a_r.at[1])
    total = own[place]
    for i in range(15):
        total = total + rxy[i].astype(F32)

    for q in range(4):
        zown[:, q, :] = total[:, q * 128 : (q + 1) * 128]
    for i in range(1, 16):
        pz = z_peer(i)
        send(zown.at[pz], rz.at[i - 1], a_s.at[2], a_r.at[2], device(x, lax.rem(pz, 4), k, pz // 4, y))
    wait(rz, a_r.at[2])
    done = zown[z]
    for i in range(15):
        done = done + rz[i]

    gz[z] = done
    for i in range(1, 16):
        pz = z_peer(i)
        send(gz.at[z], gz.at[z], a_s.at[3], a_r.at[3], device(x, lax.rem(pz, 4), k, pz // 4, y))
    wait(gz.at[pl.ds(0, 15)], a_r.at[3])
    here = k * 16 + place
    for q in range(4):
        gxy[here, :, q * 128 : (q + 1) * 128] = gz[:, q, :].astype(BF)
    for i in range(1, 16):
        px, py = xy_peer(i)
        send(gxy.at[here], gxy.at[here], a_s.at[4], a_r.at[4], device(px, zl, k, zh, py))
    wait(gxy.at[pl.ds(0, 15)], a_r.at[4])
    ref = gxy.at[pl.ds(k * 16, 16)]
    send(ref, ref, a_s.at[5], a_r.at[5], sibling)

    for f in range(C):
        wait(ag[f].at[pl.ds(0, 3)], zs.at[f])
        wait(ag[f].at[pl.ds(0, 8)], xs.at[f])
        wait(ag[f].at[pl.ds(0, 4)], fs.at[f])
        wait(ag[f].at[pl.ds(0, 16)], cs.at[f])
        wait(te[f].at[pl.ds(0, 4)], ys.at[f])
        wait(te[f].at[pl.ds(0, 8)], ys2.at[f])
        wait(sb[f].at[0], zs1.at[f])
        wait(sb[f].at[pl.ds(0, 2)], zs2.at[f])
    wait(sib, a_s.at[0])
    wait(rxy, a_s.at[1])
    wait(rz, a_s.at[2])
    wait(gz.at[pl.ds(0, 15)], a_s.at[3])
    wait(gxy.at[pl.ds(0, 15)], a_s.at[4])
    wait(ref, a_s.at[5])
    wait(ref, a_r.at[5])
    grad_out[...] = gxy[...].reshape(W, W)


def local(features, weight, edge_tiles, tile_col, tile_count, cotangent):
    vm = pltpu.VMEM
    scratch = []
    for shape, kind in (
        ((32, N), BF), ((16, N), BF), ((2, 2, N), BF), ((2, 4, N), BF),
        ((4, N), F32), ((4, N), BF), ((2, 64), BF), ((2, N), BF),
    ):
        scratch += [vm((*shape, w), kind) for _, w in CHUNKS]
    scratch += [
        vm((16, 3, N, N), BF), vm((16, N, 3 * N), BF), vm((N, W), BF), vm((W, W), BF), vm((N, W), BF), vm((N, W), BF),
        vm((16, 16, W), F32), vm((16, 16, W), BF), vm((16, 16, W), BF), vm((16, 16, W), BF), vm((15, 16, W), BF),
        vm((16, 4, 128), F32), vm((15, 4, 128), F32), vm((16, 4, 128), F32), vm((32, 16, W), BF),
    ]
    dma = pltpu.SemaphoreType.DMA
    scratch += [
        dma((C + 3,)), dma((C,)), dma((C,)), dma((C,)), dma((C, 2)), dma((C,)), dma((C,)), dma((C,)), dma((C,)),
        dma((C,)), dma((C, 2)), dma((C,)), dma((C,)), dma((C,)), dma((C, 2)), dma((C,)), dma((C,)), dma((6,)), dma((6,)),
    ]
    smem, any_, vmem = (pl.BlockSpec(memory_space=m) for m in (pltpu.SMEM, pl.ANY, pltpu.VMEM))
    activations, grad = pl.pallas_call(
        kernel,
        name="conv",
        out_shape=(jax.ShapeDtypeStruct((N, W), BF), jax.ShapeDtypeStruct((W, W), BF)),
        in_specs=[smem, smem, any_, any_, any_, any_],
        out_specs=(vmem, vmem),
        scratch_shapes=scratch,
        compiler_params=pltpu.CompilerParams(
            collective_id=0, has_side_effects=True, vmem_limit_bytes=40 * 2**20
        ),
    )(tile_count[0], tile_col[0, 0], features, edge_tiles[0, 0], cotangent, weight)
    return activations, grad.astype(F32)


def solution(mesh):
    return jax.shard_map(
        local,
        mesh=mesh,
        in_specs=(
            P(("row", "col"), None),
            P(),
            P("row", "col", None, None, None, None),
            P("row", "col", None, None),
            P("row", "col", None),
            P(("row", "col"), None),
        ),
        out_specs=(P(("row", "col"), None), P()),
        check_vma=False,
    )
```

time: 705 us -> 112 us (0.16)
  waiting for transfers between devices: 663 us -> 0 us
  Pallas kernels: 0 us -> 104 us
  between operations: 13.8 us -> 0.64 us
  local copies, waits for them, and re-layouts: 17.9 us -> 6.32 us
  matrix products: 9.59 us -> 0 us
    psum x1 -> x0, waiting for transfers between devices: 465 us -> none  [local(): weight_grad = lax.psum(grad_term, ('row', 'col'))]
    reduce_scatter x1 -> x0, waiting for transfers between devices: 125 us -> none  [local(): lax.psum_scatter(rounded_terms, 'col', scatter_dimension=0, tiled=True)]
    pallas_call x0 -> x1, Pallas kernels: none -> 104 us  [local(): pl.pallas_call(kernel, name='conv', out_shape=(jax.ShapeDtypeStruct((N, W...]
    all_gather x1 -> x0, waiting for transfers between devices: 72.5 us -> none  [local(): gathered = lax.all_gather(features, 'row', axis=0, tiled=True)]
    gather x3 -> x0, local copies, waits for them, and re-layouts: 11.3 us -> none  [local(): picked = node_blocks[column_ids[:, slot]]]
    dot_general x5 -> x0, matrix products: 9.59 us -> none  [the longest x3 5.5 us: local(): jnp.einsum('aij,ajf->aif', local_tiles[:, slot], picked, preferred_elemen...]
  transfers between devices with their start and end apart: 3 -> 0, of which waited for: 3 -> 0; matrix products, arithmetic and copies ran while one was open for 0% -> 0% of each run, Pallas kernels for 0% -> 0%
where the time goes in v1:
time: 112 us
  Pallas kernels  104 us (93%)
  local copies, waits for them, and re-layouts  6.32 us (6%)
    pallas_call x1, Pallas kernels, local(): pl.pallas_call(kernel, name='conv', out_shape=(jax.ShapeDtypeStruct((N, W...  104 us
    unnamed x11, local copies, waits for them, and re-layouts  5.57 us

profile of v1, /device:TPU:1, one launch (start us, length us, event | category | flops | bytes accessed | tf_op | source)
XLA Modules:
  0.0 112.1 jit_solution(3249259484744691774)
XLA Ops:
  0.6 0.8 copy.9
  1.4 0.0 copy-start
  1.4 1.4 %copy-done = bf16[1,1,16,3,128,128]{5,4,3,2,1,0:T(8,128)(2,1)S(1)} copy-done((bf16[1,1,16,3,128,128]{5,4,3,2,1,0:T(8,128)(2,1)S(1)}, bf16[1,1,16,3,128,128]{5,4,3,2,1,0:T(8,128)(2,1)}, u32[]{:S(2)}) %copy-start) | copy-done | bytes 1572888
  2.8 0.0 copy-start.1
  2.8 1.0 copy-done.1
  3.8 0.0 copy-start.2
  3.8 0.9 copy-done.2
  4.7 0.0 copy-start.3
  4.7 0.9 copy-done.3
  5.6 0.0 copy-start.4
  5.6 0.7 copy-done.4
  6.3 104.1 %conv.1 = (bf16[128,512]{1,0:T(8,128)(2,1)S(1)}, bf16[512,512]{1,0:T(8,128)(2,1)S(1)}) custom-call(s32[1,16]{1,0:T(1,128)S(1)} %bitcast.5, s32[16,3]{1,0:T(8,128)S(1)} %bitcast.4, bf16[128,512]{1,0:T(8,128)(2,1)S(1)} %copy-done.2, bf16[16,3,128,128]{3,2,1,0:T(8,128)(2,1)S(1)} %bitcast.3, bf16[128,512]{1,0:T(8,128)(2,1)S(1)} %copy-done.3, ...), custom_call_target="tpu_custom_call" | custom-call | tf_op jit(solution)/shard_map/conv/pallas_call | solution.py:298
  110.4 1.1 convert_element_type.3
  111.5 0.7 copy.11
Async XLA Ops:
  1.4 1.4 %copy-start = (bf16[1,1,16,3,128,128]{5,4,3,2,1,0:T(8,128)(2,1)S(1)}, bf16[1,1,16,3,128,128]{5,4,3,2,1,0:T(8,128)(2,1)}, u32[]{:S(2)}) copy-start(bf16[1,1,16,3,128,128]{5,4,3,2,1,0:T(8,128)(2,1)} %param.8) | copy-start | bytes 4718596
  2.8 1.0 copy-start.1
  3.8 0.9 copy-start.2
  4.7 0.9 copy-start.3
  5.6 0.7 copy-start.4

commit v2 on v0

v2 whole, which is shorter than its diff:
```python
import jax
import jax.numpy as jnp
from jax import lax
from jax.experimental import pallas as pl
from jax.experimental.pallas import tpu as pltpu
from jax.sharding import PartitionSpec as P

MESH = pl.DeviceIdType.MESH
BF, F32 = jnp.bfloat16, jnp.float32
N, W = 128, 512
CHUNKS = ((0, 128), (128, 128), (256, 128), (384, 128))
C = len(CHUNKS)
PIECES = ((0, 0, 128), (1, 0, 128), (2, 0, 128), (3, 0, 64), (3, 64, 64))
NP = len(PIECES)
ORDER = (
    ("own", 0), ("own", 1), ("own", 2), ("own", 3), ("line", 0), ("line", 1), ("on", 0, 0), ("on", 1, 0),
    ("ring", 0, 1), ("on", 2, 0), ("on", 3, 0), ("ring", 0, 2), ("line", 2), ("end", 0, 0), ("ring", 1, 1),
    ("end", 1, 0), ("ring", 0, 3), ("on", 0, 1), ("end", 2, 0), ("ring", 1, 2), ("line", 3), ("end", 3, 0),
    ("on", 0, 2), ("ring", 2, 1), ("ring", 1, 3), ("on", 1, 1), ("on", 0, 3), ("ring", 2, 2), ("end", 0, 1),
    ("on", 1, 2), ("ring", 3, 1), ("end", 0, 2), ("ring", 2, 3), ("on", 2, 1), ("on", 1, 3), ("ring", 3, 2),
    ("end", 1, 1), ("end", 0, 3), ("end", 1, 2), ("on", 2, 2), ("ring", 3, 3), ("mul", 0, 0), ("on", 3, 1),
    ("mul", 0, 1), ("on", 2, 3), ("mul", 0, 2), ("end", 2, 1), ("mul", 0, 3), ("end", 1, 3), ("on", 3, 2),
    ("end", 2, 2), ("mul", 1, 0), ("on", 3, 3), ("mul", 1, 1), ("end", 3, 1), ("mul", 1, 2), ("y", 0),
    ("end", 2, 3), ("mul", 1, 3), ("end", 3, 2), ("mul", 2, 0), ("mul", 2, 1), ("end", 3, 3), ("mul", 2, 2),
    ("mul", 2, 3), ("y", 1), ("mul", 3, 0), ("mul", 3, 1), ("mul", 3, 2), ("mul", 3, 3), ("y_end", 0), ("y", 2),
    ("y_end", 1), ("y", 3), ("y", 4), ("z", 0), ("y_end", 2), ("y_end", 3), ("y_end", 4), ("z", 1), ("z_end", 0),
    ("z", 2), ("z", 3), ("z", 4), ("z_end", 1), ("z_end", 2), ("z_end", 3), ("z_end", 4),
)


def device(x, zl, k, zh, y):
    return ((x * 4 + zl) * 2 + k, zh * 4 + y)


def turn(value, by):
    return lax.rem(value + (by + 16), 4)


def far(offset):
    dx, dy = offset // 4, offset % 4
    return min(dx, 4 - dx) + min(dy, 4 - dy)


NEAR_FIRST = sorted(range(1, 16), key=far)


def kernel(
    count_ref, col_ref, feat, edges, cot, weight, act_out, grad_out,
    *scratch,
):
    ag, te = scratch[:C], scratch[C : 2 * C]
    r1, r2, su, sb, r3, r4 = (scratch[2 * C + i * NP : 2 * C + (i + 1) * NP] for i in range(6))
    (raw, em, cv, wv, av, gv, own, sib, rsib, part, rxy, hi, lo, gxy,
     in_sem, zs, zr, xs, xr, fs, fr, cs, cr, ys, yr, ys2, yr2, zs1, zr1, zs2, zr2, a_s, a_r, g_r) = scratch[2 * C + 6 * NP :]
    row, col = lax.axis_index("row"), lax.axis_index("col")
    x, zl, k = row // 8, lax.rem(row // 2, 4), lax.rem(row, 2)
    zh, y = col // 4, lax.rem(col, 4)
    sibling = device(x, zl, 1 - k, zh, y)
    right, left = device(turn(x, 1), zl, k, zh, y), device(turn(x, -1), zl, k, zh, y)
    up, down = device(x, zl, k, zh, turn(y, 1)), device(x, zl, k, zh, turn(y, -1))
    above, below = device(x, zl, k, turn(zh, 1), y), device(x, zl, k, turn(zh, -1), y)
    line = [device(x, turn(zl, d), k, zh, y) for d in (1, 2, 3)]
    first, last = 1 + lax.rem(zl, 2), 3 * (1 - zl // 2)
    places = (zl, first, 6 - zl - first - last, last)

    def slot(core, at_x, at_zl=0):
        return core * 16 + at_x * 4 + at_zl

    def send(src, dst, send_sem, recv_sem, to):
        pltpu.make_async_remote_copy(
            src_ref=src, dst_ref=dst, send_sem=send_sem, recv_sem=recv_sem, device_id=to, device_id_type=MESH
        ).start()

    def wait(ref, sem):
        pltpu.make_async_copy(ref, ref, sem).wait()

    loads = [
        pltpu.make_async_copy(feat.at[:, s : s + w], ag[f].at[slot(k, x, zl)], in_sem.at[f])
        for f, (s, w) in enumerate(CHUNKS)
    ]
    loads += [
        pltpu.make_async_copy(edges, raw, in_sem.at[C]),
        pltpu.make_async_copy(weight, wv, in_sem.at[C + 1]),
        pltpu.make_async_copy(cot, cv, in_sem.at[C + 2]),
    ]
    for load in loads:
        load.start()

    barrier = pltpu.get_barrier_semaphore()
    partners = [*line, above, below, right, left, up, down, sibling]
    for to in partners:
        pl.semaphore_signal(barrier, inc=1, device_id=to, device_id_type=MESH)
    pl.semaphore_wait(barrier, len(partners))

    def to_ring(f, i):
        ref = ag[f].at[slot(k, x, places[i])]
        send(ref, ref, xs.at[f], xr.at[f, 0, i], right)
        send(ref, ref, xs.at[f], xr.at[f, 1, i], left)
        send(ref, ref, cs.at[f], cr.at[f], sibling)

    def gather_own(f):
        loads[f].wait()
        to_ring(f, 0)

    def gather_line(f):
        ref = ag[f].at[slot(k, x, zl)]
        for to in line:
            send(ref, ref, zs.at[f], zr.at[f, zl], to)

    def gather_ring(f, i):
        wait(ag[f].at[slot(k, x, places[i])], zr.at[f, places[i]])
        to_ring(f, i)

    def gather_on(f, i):
        refs = [ag[f].at[slot(k, turn(x, d), places[i])] for d in (-1, 1)]
        for d in (i % 2, 1 - i % 2):
            wait(refs[d], xr.at[f, d, i])
            if d == i % 2:
                send(refs[d], refs[d], fs.at[f], fr.at[f, i], left if d else right)
            send(refs[d], refs[d], cs.at[f], cr.at[f], sibling)

    def gather_end(f, i):
        ref = ag[f].at[slot(k, turn(x, 2), places[i])]
        wait(ref, fr.at[f, i])
        send(ref, ref, cs.at[f], cr.at[f], sibling)

    def mask_tiles():
        loads[C].wait()

        def one(a, _):
            count = count_ref[0, a]
            for s in range(3):
                tile = raw[a, s]
                em[a, :, s * N : (s + 1) * N] = jnp.where(s < count, tile, jnp.zeros_like(tile))
            return _

        lax.fori_loop(0, 16, one, 0)

    def terms(f, to_y):
        for q in range(4):
            a = q * 4 + to_y
            picked = []
            for s in range(3):
                j = col_ref[s, 0, a]
                picked.append(ag[f][lax.rem(j, 2) * 16 + j // 2])
            made = jnp.dot(em[a], jnp.concatenate(picked, axis=0), preferred_element_type=F32)
            te[f][to_y * 4 + q] = made.astype(BF)

    y_up, y_down, y_far = turn(y, 1), turn(y, -1), turn(y, 2)

    def multiply(f, group):
        if group == 0:
            wait(ag[f].at[pl.ds(0, 16)], cr.at[f])
        terms(f, (y_far, y_up, y_down, y)[group])
        for p, (chunk, r, n) in enumerate(PIECES):
            rows = pl.ds(r, n)
            if chunk != f:
                continue
            if group == 0:
                send(te[f].at[pl.ds(y_far * 4, 2), rows], r1[p].at[0], ys.at[p], yr.at[p, 0], up)
                send(te[f].at[pl.ds(y_far * 4 + 2, 2), rows], r1[p].at[1], ys.at[p], yr.at[p, 1], down)
            if group == 1:
                send(te[f].at[pl.ds(y_up * 4 + 2, 2), rows], r2[p].at[0, pl.ds(2, 2)], ys2.at[p], yr2.at[p], up)
            if group == 2:
                send(te[f].at[pl.ds(y_down * 4, 2), rows], r2[p].at[1, pl.ds(0, 2)], ys2.at[p], yr2.at[p], down)

    def reduce_y(p):
        f, r, n = PIECES[p]
        for d, at, to in ((0, y_up * 4, up), (1, y_down * 4 + 2, down)):
            wait(r1[p].at[d], yr.at[p, d])
            ref = te[f].at[pl.ds(at, 2), pl.ds(r, n)]
            ref[...] = (ref[...].astype(F32) + r1[p][d].astype(F32)).astype(BF)
            send(ref, r2[p].at[d, pl.ds(2 * d, 2)], ys2.at[p], yr2.at[p], to)

    z_up, z_down, z_far = turn(zh, 1), turn(zh, -1), turn(zh, 2)

    def reduce_y_end(p):
        f, r, n = PIECES[p]
        wait(r2[p], yr2.at[p])

        def total(q):
            return te[f][y * 4 + q, r : r + n].astype(F32) + r2[p][0, q].astype(F32) + r2[p][1, q].astype(F32)

        sb[p][z_far] = total(z_far).astype(BF)
        send(sb[p].at[z_far, pl.ds(0, n // 2)], r3[p].at[0], zs1.at[p], zr1.at[p, 0], above)
        send(sb[p].at[z_far, pl.ds(n // 2, n // 2)], r3[p].at[1], zs1.at[p], zr1.at[p, 1], below)
        for q in (z_up, z_down, zh):
            su[p][q] = total(q)

    def reduce_z(p):
        h = PIECES[p][2] // 2
        for d, at, to in ((0, z_up, above), (1, z_down, below)):
            wait(r3[p].at[d], zr1.at[p, d])
            add, keep = pl.ds(d * h, h), pl.ds((1 - d) * h, h)
            sb[p][at, add] = (su[p][at, add] + r3[p][d].astype(F32)).astype(BF)
            sb[p][at, keep] = su[p][at, keep].astype(BF)
            send(sb[p].at[at], r4[p].at[d], zs2.at[p], zr2.at[p], to)

    def sent():
        for f in range(C):
            wait(ag[f].at[pl.ds(0, 3)], zs.at[f])
            wait(ag[f].at[pl.ds(0, 8)], xs.at[f])
            wait(ag[f].at[pl.ds(0, 4)], fs.at[f])
            wait(ag[f].at[pl.ds(0, 16)], cs.at[f])
        for p in range(NP):
            wait(r1[p], ys.at[p])
            wait(r2[p], ys2.at[p])
            wait(r3[p], zs1.at[p])
            wait(r4[p], zs2.at[p])

    def reduce_z_end(p):
        f, r, n = PIECES[p]
        s, w = CHUNKS[f]
        if p == NP - 1:
            sent()
            loads[C + 1].wait()
            loads[C + 2].wait()
        wait(r4[p], zr2.at[p])
        av[r : r + n, s : s + w] = (su[p][zh] + r4[p][0].astype(F32) + r4[p][1].astype(F32)).astype(BF)

    steps = {
        "own": gather_own, "line": gather_line, "ring": gather_ring, "on": gather_on, "end": gather_end, "mul": multiply,
        "y": reduce_y, "y_end": reduce_y_end, "z": reduce_z, "z_end": reduce_z_end,
    }
    for step, *which in ORDER:
        if (step, *which) == ("on", 0, 0):
            mask_tiles()
        steps[step](*which)

    preact = jnp.dot(av[...], wv[...], preferred_element_type=F32)
    sig = jax.nn.sigmoid(preact)
    gv[...] = (cv[...].astype(F32) * sig * (1.0 + preact * (1.0 - sig))).astype(BF)
    act_out[...] = (preact * sig).astype(BF)

    def share(half):
        rows = av[:, pl.ds(pl.multiple_of(half * 256, 256), 256)]
        made = lax.dot_general(rows, gv[...], (((0,), (0,)), ((), ())), preferred_element_type=F32)
        return made.reshape(16, 16, W)

    sib[...] = share(1 - k).astype(BF)
    send(sib, rsib, a_s.at[0], a_r.at[0], sibling)
    own[...] = share(k)
    wait(rsib, a_r.at[0])
    own[...] = own[...] + rsib[...].astype(F32)
    part[...] = own[...].astype(BF)

    place = x * 4 + y

    def peer(i):
        return turn(x, i // 4), turn(y, i % 4)

    for i in reversed(NEAR_FIRST):
        px, py = peer(i)
        send(part.at[px * 4 + py], rxy.at[i - 1], a_s.at[1], a_r.at[1], device(px, zl, k, zh, py))
    wait(rxy, a_r.at[1])
    total = own[place]
    for i in range(15):
        total = total + rxy[i].astype(F32)

    def exchange(buf, at, stage, to):
        buf[at] = total.astype(BF)
        for d in (2, 1, 3):
            send(buf.at[at], buf.at[at], a_s.at[stage], a_r.at[stage], to(d))
        wait(buf.at[pl.ds(0, 3)], a_r.at[stage])
        return sum(buf[i].astype(F32) for i in range(4))

    total = exchange(hi, zh, 2, lambda d: device(x, zl, k, turn(zh, d), y))
    total = exchange(lo, zl, 3, lambda d: line[d - 1])

    here = k * 16 + place
    gxy[here] = total.astype(BF)
    send(gxy.at[here], gxy.at[here], a_s.at[5], a_r.at[5], sibling)
    for i in reversed(NEAR_FIRST):
        px, py = peer(i)
        send(gxy.at[here], gxy.at[here], a_s.at[4], g_r.at[i], device(px, zl, k, zh, py))
    for i in NEAR_FIRST:
        ref = gxy.at[k * 16 + turn(x, -(i // 4)) * 4 + turn(y, -(i % 4))]
        wait(ref, g_r.at[i])
        send(ref, ref, a_s.at[5], a_r.at[5], sibling)

    wait(sib, a_s.at[0])
    wait(rxy, a_s.at[1])
    wait(hi.at[pl.ds(0, 3)], a_s.at[2])
    wait(lo.at[pl.ds(0, 3)], a_s.at[3])
    wait(rxy, a_s.at[4])
    wait(part, a_s.at[5])
    wait(part, a_r.at[5])
    grad_out[...] = gxy[...].reshape(W, W)


def local(features, weight, edge_tiles, tile_col, tile_count, cotangent):
    vm = pltpu.VMEM
    scratch = []
    for rows in (32, 16):
        scratch += [vm((rows, N, w), BF) for _, w in CHUNKS]
    for shape, part, kind in (((2, 2), 1, BF), ((2, 4), 1, BF), ((4,), 1, F32), ((4,), 1, BF), ((2,), 2, BF), ((2,), 1, BF)):
        scratch += [vm((*shape, n // part, CHUNKS[f][1]), kind) for f, _, n in PIECES]
    scratch += [
        vm((16, 3, N, N), BF), vm((16, N, 3 * N), BF), vm((N, W), BF), vm((W, W), BF), vm((N, W), BF), vm((N, W), BF),
        vm((16, 16, W), F32), vm((16, 16, W), BF), vm((16, 16, W), BF), vm((16, 16, W), BF), vm((15, 16, W), BF),
        vm((4, 16, W), BF), vm((4, 16, W), BF), vm((32, 16, W), BF),
    ]
    for shape in (
        (C + 3,), (C,), (C, 4), (C,), (C, 2, 4), (C,), (C, 4), (C,), (C,),
        (NP,), (NP, 2), (NP,), (NP,), (NP,), (NP, 2), (NP,), (NP,), (6,), (6,), (16,),
    ):
        scratch.append(pltpu.SemaphoreType.DMA(shape))
    smem, any_, vmem = (pl.BlockSpec(memory_space=m) for m in (pltpu.SMEM, pl.ANY, pltpu.VMEM))
    activations, grad = pl.pallas_call(
        kernel,
        name="conv",
        out_shape=(jax.ShapeDtypeStruct((N, W), BF), jax.ShapeDtypeStruct((W, W), BF)),
        in_specs=[smem, smem, any_, any_, any_, any_],
        out_specs=(vmem, vmem),
        scratch_shapes=scratch,
        compiler_params=pltpu.CompilerParams(
            collective_id=0, has_side_effects=True, vmem_limit_bytes=60 * 2**20
        ),
    )(tile_count[0], jnp.transpose(tile_col, (0, 3, 1, 2))[0], features, edge_tiles[0, 0], cotangent, weight)
    return activations, grad.astype(F32)


def solution(mesh):
    return jax.shard_map(
        local,
        mesh=mesh,
        in_specs=(
            P(("row", "col"), None),
            P(),
            P("row", "col", None, None, None, None),
            P("row", "col", None, None),
            P("row", "col", None),
            P(("row", "col"), None),
        ),
        out_specs=(P(("row", "col"), None), P()),
        check_vma=False,
    )
```

time: 705 us -> 99.1 us (0.14)
  waiting for transfers between devices: 663 us -> 0 us
  Pallas kernels: 0 us -> 95.5 us
  local copies, waits for them, and re-layouts: 17.9 us -> 0.66 us
  between operations: 13.8 us -> 0.65 us
  matrix products: 9.59 us -> 0 us
    psum x1 -> x0, waiting for transfers between devices: 465 us -> none  [local(): weight_grad = lax.psum(grad_term, ('row', 'col'))]
    reduce_scatter x1 -> x0, waiting for transfers between devices: 125 us -> none  [local(): lax.psum_scatter(rounded_terms, 'col', scatter_dimension=0, tiled=True)]
    pallas_call x0 -> x1, Pallas kernels: none -> 95.5 us  [local(): pl.pallas_call(kernel, name='conv', out_shape=(jax.ShapeDtypeStruct((N, W...]
    all_gather x1 -> x0, waiting for transfers between devices: 72.5 us -> none  [local(): gathered = lax.all_gather(features, 'row', axis=0, tiled=True)]
    gather x3 -> x0, local copies, waits for them, and re-layouts: 11.3 us -> none  [local(): picked = node_blocks[column_ids[:, slot]]]
    dot_general x5 -> x0, matrix products: 9.59 us -> none  [the longest x3 5.5 us: local(): jnp.einsum('aij,ajf->aif', local_tiles[:, slot], picked, preferred_elemen...]
  transfers between devices with their start and end apart: 3 -> 0, of which waited for: 3 -> 0; matrix products, arithmetic and copies ran while one was open for 0% -> 0% of each run, Pallas kernels for 0% -> 0%
where the time goes in v2:
time: 99.1 us; the launch traced here: 99 us
  Pallas kernels  95.5 us (96%)
  other arithmetic  2.18 us (2%)
    pallas_call x1, Pallas kernels, local(): pl.pallas_call(kernel, name='conv', out_shape=(jax.ShapeDtypeStruct((N, W...  95.5 us
    convert_element_type x1, other arithmetic, local(): return (activations, grad.astype(F32))  2.18 us

profile of v2, /device:TPU:1, one launch (start us, length us, event | category | flops | bytes accessed | tf_op | source)
XLA Modules:
  0.0 99.0 jit_solution(5303086642148196418)
XLA Ops:
  0.6 95.5 %conv.1 = (bf16[128,512]{1,0:T(8,128)(2,1)}, bf16[512,512]{1,0:T(8,128)(2,1)}) custom-call(s32[1,16]{1,0:T(1,128)} %bitcast.7, s32[3,1,16]{2,1,0:T(1,128)} %bitcast.6, bf16[128,512]{1,0:T(8,128)(2,1)} %feat.1, bf16[16,3,128,128]{3,2,1,0:T(8,128)(2,1)} %bitcast.5, bf16[128,512]{1,0:T(8,128)(2,1)} %cot.1, bf16[512,512]{1,0:T(8,128)(2,1)} %weight.1), custom_call_target="tpu_custom_call" | custom-call | tf_op jit(solution)/shard_map/conv/pallas_call | solution.py:309
  96.1 0.0 copy-start
  96.1 2.2 %convert_element_type.3 = f32[512,512]{1,0:T(8,128)} convert(bf16[512,512]{1,0:T(8,128)(2,1)} %get-tuple-element.5) | non-fusion elementwise | flops 262144 | bytes 1572864 | tf_op jit(solution)/shard_map/convert_element_type | solution.py:320
  98.3 0.0 copy-done
  98.3 0.7 copy.9
Async XLA Ops:
  96.1 2.2 %copy-start = (bf16[128,512]{1,0:T(8,128)(2,1)S(1)}, bf16[128,512]{1,0:T(8,128)(2,1)}, u32[]{:S(2)}) copy-start(bf16[128,512]{1,0:T(8,128)(2,1)} %get-tuple-element.8) | copy-start | bytes 393220

commit v3 on v2

--- a/solution.py
+++ b/solution.py
@@ -10,22 +10,32 @@
 N, W = 128, 512
 CHUNKS = ((0, 128), (128, 128), (256, 128), (384, 128))
 C = len(CHUNKS)
-PIECES = ((0, 0, 128), (1, 0, 128), (2, 0, 128), (3, 0, 64), (3, 64, 64))
+PIECES = tuple((f, r, 64) for f in range(C) for r in (0, 64))
 NP = len(PIECES)
-ORDER = (
-    ("own", 0), ("own", 1), ("own", 2), ("own", 3), ("line", 0), ("line", 1), ("on", 0, 0), ("on", 1, 0),
-    ("ring", 0, 1), ("on", 2, 0), ("on", 3, 0), ("ring", 0, 2), ("line", 2), ("end", 0, 0), ("ring", 1, 1),
-    ("end", 1, 0), ("ring", 0, 3), ("on", 0, 1), ("end", 2, 0), ("ring", 1, 2), ("line", 3), ("end", 3, 0),
-    ("on", 0, 2), ("ring", 2, 1), ("ring", 1, 3), ("on", 1, 1), ("on", 0, 3), ("ring", 2, 2), ("end", 0, 1),
-    ("on", 1, 2), ("ring", 3, 1), ("end", 0, 2), ("ring", 2, 3), ("on", 2, 1), ("on", 1, 3), ("ring", 3, 2),
-    ("end", 1, 1), ("end", 0, 3), ("end", 1, 2), ("on", 2, 2), ("ring", 3, 3), ("mul", 0, 0), ("on", 3, 1),
-    ("mul", 0, 1), ("on", 2, 3), ("mul", 0, 2), ("end", 2, 1), ("mul", 0, 3), ("end", 1, 3), ("on", 3, 2),
-    ("end", 2, 2), ("mul", 1, 0), ("on", 3, 3), ("mul", 1, 1), ("end", 3, 1), ("mul", 1, 2), ("y", 0),
-    ("end", 2, 3), ("mul", 1, 3), ("end", 3, 2), ("mul", 2, 0), ("mul", 2, 1), ("end", 3, 3), ("mul", 2, 2),
-    ("mul", 2, 3), ("y", 1), ("mul", 3, 0), ("mul", 3, 1), ("mul", 3, 2), ("mul", 3, 3), ("y_end", 0), ("y", 2),
-    ("y_end", 1), ("y", 3), ("y", 4), ("z", 0), ("y_end", 2), ("y_end", 3), ("y_end", 4), ("z", 1), ("z_end", 0),
-    ("z", 2), ("z", 3), ("z", 4), ("z_end", 1), ("z_end", 2), ("z_end", 3), ("z_end", 4),
-)
+
+
+def of(step, f, first=1):
+    return [(step, f, i) for i in range(first, 4)]
+
+
+def pieces(step, f):
+    return [(step, p) for p in range(NP) if PIECES[p][0] == f]
+
+
+def mixed(*lists):
+    return [each[i] for i in range(max(map(len, lists))) for each in lists if i < len(each)]
+
+
+ORDER = [
+    ("own", 0), ("line", 0), ("own", 1), ("line", 1), ("own", 2), ("line", 2), ("own", 3), ("line", 3),
+    ("on", 0, 0), ("on", 1, 0), ("on", 2, 0), ("on", 3, 0),
+    *of("ring", 0), *of("ring", 1), *of("on", 0), *of("ring", 2), *of("on", 1), *of("ring", 3),
+    *of("end", 0, 0), *mixed(of("mul", 0, 0), of("on", 2)), *of("end", 1, 0), *mixed(of("mul", 1, 0), of("on", 3)),
+    *pieces("y", 0), *of("end", 2, 0), *of("mul", 2, 0), *pieces("y", 1), *pieces("y_end", 0),
+    *of("end", 3, 0), *of("mul", 3, 0), *pieces("y", 2), *pieces("y_end", 1), *pieces("z", 0),
+    *pieces("y", 3), *pieces("y_end", 2), *pieces("y_end", 3), *pieces("z", 1), *pieces("z_end", 0),
+    *pieces("z", 2), *pieces("z", 3), *pieces("z_end", 1), *pieces("z_end", 2), *pieces("z_end", 3),
+]
 
 
 def device(x, zl, k, zh, y):
@@ -92,11 +102,16 @@
         pl.semaphore_signal(barrier, inc=1, device_id=to, device_id_type=MESH)
     pl.semaphore_wait(barrier, len(partners))
 
+    def to_sibling(f, at_x):
+        ref = ag[f].at[pl.ds(slot(k, at_x), 4)]
+        send(ref, ref, cs.at[f], cr.at[f], sibling)
+
     def to_ring(f, i):
         ref = ag[f].at[slot(k, x, places[i])]
         send(ref, ref, xs.at[f], xr.at[f, 0, i], right)
         send(ref, ref, xs.at[f], xr.at[f, 1, i], left)
-        send(ref, ref, cs.at[f], cr.at[f], sibling)
+        if i == 3:
+            to_sibling(f, x)
 
     def gather_own(f):
         loads[f].wait()
@@ -108,7 +123,8 @@
             send(ref, ref, zs.at[f], zr.at[f, zl], to)
 
     def gather_ring(f, i):
-        wait(ag[f].at[slot(k, x, places[i])], zr.at[f, places[i]])
+        ref = ag[f].at[slot(k, x, places[i])]
+        wait(ref, zr.at[f, places[i]])
         to_ring(f, i)
 
     def gather_on(f, i):
@@ -117,12 +133,14 @@
             wait(refs[d], xr.at[f, d, i])
             if d == i % 2:
                 send(refs[d], refs[d], fs.at[f], fr.at[f, i], left if d else right)
-            send(refs[d], refs[d], cs.at[f], cr.at[f], sibling)
+            if i == 3:
+                to_sibling(f, turn(x, (-1, 1)[d]))
 
     def gather_end(f, i):
         ref = ag[f].at[slot(k, turn(x, 2), places[i])]
         wait(ref, fr.at[f, i])
-        send(ref, ref, cs.at[f], cr.at[f], sibling)
+        if i == 3:
+            to_sibling(f, turn(x, 2))
 
     def mask_tiles():
         loads[C].wait()
@@ -305,12 +323,12 @@
         (NP,), (NP, 2), (NP,), (NP,), (NP,), (NP, 2), (NP,), (NP,), (6,), (6,), (16,),
     ):
         scratch.append(pltpu.SemaphoreType.DMA(shape))
-    smem, any_, vmem = (pl.BlockSpec(memory_space=m) for m in (pltpu.SMEM, pl.ANY, pltpu.VMEM))
+    smem, hbm, vmem = (pl.BlockSpec(memory_space=m) for m in (pltpu.SMEM, pltpu.HBM, pltpu.VMEM))
     activations, grad = pl.pallas_call(
         kernel,
         name="conv",
         out_shape=(jax.ShapeDtypeStruct((N, W), BF), jax.ShapeDtypeStruct((W, W), BF)),
-        in_specs=[smem, smem, any_, any_, any_, any_],
+        in_specs=[smem, smem, hbm, hbm, hbm, hbm],
         out_specs=(vmem, vmem),
         scratch_shapes=scratch,
         compiler_params=pltpu.CompilerParams(

time: 99.1 us -> 97.2 us (0.981)
  Pallas kernels: 95.5 us -> 93.5 us
    pallas_call x1, Pallas kernels: 95.5 us -> 93.5 us  [local(): pl.pallas_call(kernel, name='conv', out_shape=(jax.ShapeDtypeStruct((N, W...]
where the time goes in v3:
time: 97.2 us; the launch traced here: 97 us
  Pallas kernels  93.5 us (96%)
  other arithmetic  2.18 us (2%)
    pallas_call x1, Pallas kernels, local(): pl.pallas_call(kernel, name='conv', out_shape=(jax.ShapeDtypeStruct((N, W...  93.5 us
    convert_element_type x1, other arithmetic, local(): return (activations, grad.astype(F32))  2.18 us

profile of v3, /device:TPU:1, one launch (start us, length us, event | category | flops | bytes accessed | tf_op | source)
XLA Modules:
  0.0 97.0 jit_solution(4791023140433893745)
XLA Ops:
  0.6 93.5 %conv.1 = (bf16[128,512]{1,0:T(8,128)(2,1)}, bf16[512,512]{1,0:T(8,128)(2,1)}) custom-call(s32[1,16]{1,0:T(1,128)} %bitcast.7, s32[3,1,16]{2,1,0:T(1,128)} %bitcast.6, bf16[128,512]{1,0:T(8,128)(2,1)} %feat.1, bf16[16,3,128,128]{3,2,1,0:T(8,128)(2,1)} %bitcast.5, bf16[128,512]{1,0:T(8,128)(2,1)} %cot.1, bf16[512,512]{1,0:T(8,128)(2,1)} %weight.1), custom_call_target="tpu_custom_call" | custom-call | tf_op jit(solution)/shard_map/conv/pallas_call | solution.py:327
  94.2 0.0 copy-start
  94.2 2.2 %convert_element_type.3 = f32[512,512]{1,0:T(8,128)} convert(bf16[512,512]{1,0:T(8,128)(2,1)} %get-tuple-element.5) | non-fusion elementwise | flops 262144 | bytes 1572864 | tf_op jit(solution)/shard_map/convert_element_type | solution.py:338
  96.4 0.0 copy-done
  96.4 0.7 copy.9
Async XLA Ops:
  94.2 2.2 %copy-start = (bf16[128,512]{1,0:T(8,128)(2,1)S(1)}, bf16[128,512]{1,0:T(8,128)(2,1)}, u32[]{:S(2)}) copy-start(bf16[128,512]{1,0:T(8,128)(2,1)} %get-tuple-element.8) | copy-start | bytes 393220

commit v4 on v3

--- a/solution.py
+++ b/solution.py
@@ -259,8 +259,6 @@
     send(sib, rsib, a_s.at[0], a_r.at[0], sibling)
     own[...] = share(k)
     wait(rsib, a_r.at[0])
-    own[...] = own[...] + rsib[...].astype(F32)
-    part[...] = own[...].astype(BF)
 
     place = x * 4 + y
 
@@ -269,9 +267,10 @@
 
     for i in reversed(NEAR_FIRST):
         px, py = peer(i)
+        part[px * 4 + py] = (own[px * 4 + py] + rsib[px * 4 + py].astype(F32)).astype(BF)
         send(part.at[px * 4 + py], rxy.at[i - 1], a_s.at[1], a_r.at[1], device(px, zl, k, zh, py))
     wait(rxy, a_r.at[1])
-    total = own[place]
+    total = own[place] + rsib[place].astype(F32)
     for i in range(15):
         total = total + rxy[i].astype(F32)
 
@@ -282,8 +281,8 @@
         wait(buf.at[pl.ds(0, 3)], a_r.at[stage])
         return sum(buf[i].astype(F32) for i in range(4))
 
+    total = exchange(lo, zl, 3, lambda d: line[d - 1])
     total = exchange(hi, zh, 2, lambda d: device(x, zl, k, turn(zh, d), y))
-    total = exchange(lo, zl, 3, lambda d: line[d - 1])
 
     here = k * 16 + place
     gxy[here] = total.astype(BF)

time: 97.2 us -> 97.1 us (level)
  no operation moved by 1% of the time
where the time goes in v4:
time: 97.1 us; the launch traced here: 96.9 us
  Pallas kernels  93.4 us (96%)
  other arithmetic  2.18 us (2%)
    pallas_call x1, Pallas kernels, local(): pl.pallas_call(kernel, name='conv', out_shape=(jax.ShapeDtypeStruct((N, W...  93.4 us
    convert_element_type x1, other arithmetic, local(): return (activations, grad.astype(F32))  2.18 us

profile of v4, /device:TPU:1, one launch (start us, length us, event | category | flops | bytes accessed | tf_op | source)
XLA Modules:
  0.0 96.9 jit_solution(7292850617280697466)
XLA Ops:
  0.6 93.4 %conv.1 = (bf16[128,512]{1,0:T(8,128)(2,1)}, bf16[512,512]{1,0:T(8,128)(2,1)}) custom-call(s32[1,16]{1,0:T(1,128)} %bitcast.7, s32[3,1,16]{2,1,0:T(1,128)} %bitcast.6, bf16[128,512]{1,0:T(8,128)(2,1)} %feat.1, bf16[16,3,128,128]{3,2,1,0:T(8,128)(2,1)} %bitcast.5, bf16[128,512]{1,0:T(8,128)(2,1)} %cot.1, bf16[512,512]{1,0:T(8,128)(2,1)} %weight.1), custom_call_target="tpu_custom_call" | custom-call | tf_op jit(solution)/shard_map/conv/pallas_call | solution.py:326
  94.0 0.0 copy-start
  94.1 2.2 %convert_element_type.3 = f32[512,512]{1,0:T(8,128)} convert(bf16[512,512]{1,0:T(8,128)(2,1)} %get-tuple-element.5) | non-fusion elementwise | flops 262144 | bytes 1572864 | tf_op jit(solution)/shard_map/convert_element_type | solution.py:337
  96.2 0.0 copy-done
  96.2 0.7 copy.9
Async XLA Ops:
  94.0 2.2 %copy-start = (bf16[128,512]{1,0:T(8,128)(2,1)S(1)}, bf16[128,512]{1,0:T(8,128)(2,1)}, u32[]{:S(2)}) copy-start(bf16[128,512]{1,0:T(8,128)(2,1)} %get-tuple-element.8) | copy-start | bytes 393220

commit v5 on v4

--- a/solution.py
+++ b/solution.py
@@ -223,13 +223,11 @@
         for p in range(NP):
             wait(r1[p], ys.at[p])
             wait(r2[p], ys2.at[p])
-            wait(r3[p], zs1.at[p])
-            wait(r4[p], zs2.at[p])
 
     def reduce_z_end(p):
         f, r, n = PIECES[p]
         s, w = CHUNKS[f]
-        if p == NP - 1:
+        if p == 2:
             sent()
             loads[C + 1].wait()
             loads[C + 2].wait()
@@ -258,6 +256,9 @@
     sib[...] = share(1 - k).astype(BF)
     send(sib, rsib, a_s.at[0], a_r.at[0], sibling)
     own[...] = share(k)
+    for p in range(NP):
+        wait(r3[p], zs1.at[p])
+        wait(r4[p], zs2.at[p])
     wait(rsib, a_r.at[0])
 
     place = x * 4 + y

time: 97.1 us -> 97.1 us (level)
  no operation moved by 1% of the time
where the time goes in v5:
time: 97.1 us; the launch traced here: 96.9 us
  Pallas kernels  93.4 us (96%)
  other arithmetic  2.18 us (2%)
    pallas_call x1, Pallas kernels, local(): pl.pallas_call(kernel, name='conv', out_shape=(jax.ShapeDtypeStruct((N, W...  93.4 us
    convert_element_type x1, other arithmetic, local(): return (activations, grad.astype(F32))  2.18 us

profile of v5, /device:TPU:1, one launch (start us, length us, event | category | flops | bytes accessed | tf_op | source)
XLA Modules:
  0.0 96.9 jit_solution(11149576918494921616)
XLA Ops:
  0.6 93.4 %conv.1 = (bf16[128,512]{1,0:T(8,128)(2,1)}, bf16[512,512]{1,0:T(8,128)(2,1)}) custom-call(s32[1,16]{1,0:T(1,128)} %bitcast.7, s32[3,1,16]{2,1,0:T(1,128)} %bitcast.6, bf16[128,512]{1,0:T(8,128)(2,1)} %feat.1, bf16[16,3,128,128]{3,2,1,0:T(8,128)(2,1)} %bitcast.5, bf16[128,512]{1,0:T(8,128)(2,1)} %cot.1, bf16[512,512]{1,0:T(8,128)(2,1)} %weight.1), custom_call_target="tpu_custom_call" | custom-call | tf_op jit(solution)/shard_map/conv/pallas_call | solution.py:327
  94.0 0.0 copy-start
  94.1 2.2 %convert_element_type.3 = f32[512,512]{1,0:T(8,128)} convert(bf16[512,512]{1,0:T(8,128)(2,1)} %get-tuple-element.5) | non-fusion elementwise | flops 262144 | bytes 1572864 | tf_op jit(solution)/shard_map/convert_element_type | solution.py:338
  96.2 0.0 copy-done
  96.2 0.7 copy.9
Async XLA Ops:
  94.0 2.2 %copy-start = (bf16[128,512]{1,0:T(8,128)(2,1)S(1)}, bf16[128,512]{1,0:T(8,128)(2,1)}, u32[]{:S(2)}) copy-start(bf16[128,512]{1,0:T(8,128)(2,1)} %get-tuple-element.8) | copy-start | bytes 393220
